TPU v7x, 32 devices: a whole 2x2x4 slice. The times are simulated.
32 devices in a mesh: dp: 8 (over z, y), tensor: 4 (over x, core).
Axes of the slice: x: 2, y: 2, z: 4, core: 2. Of those that a mesh axis runs over, the one named last changes fastest.
Arguments:
- tokens: float32 [4096, 1152], P(('dp', 'tensor')), may hold values from -6 to 6
- timesteps: int32 [16], replicated, may hold values from 0 to 999
- labels: int32 [16], replicated, may hold values from 0 to 1000
- time_weight: float32 [256, 1152], P(None, 'dp'), may hold values from -0.5 to 0.5
- class_table: float32 [1001, 1152], P(None, 'dp'), may hold values from -6 to 6
- mod_weight: bfloat16 [1, 1152, 6912], P(None, 'dp', 'tensor'), may hold values from -0.1875 to 0.1875
- mod_bias: float32 [1, 6912], replicated, may hold values from -3 to 3
- qkv_weight: bfloat16 [1, 3, 1152, 1152], P(None, None, 'dp', 'tensor'), may hold values from -0.1875 to 0.1875
- qv_bias: float32 [1, 2, 1152], replicated, may hold values from -3 to 3
- proj_weight: bfloat16 [1, 1152, 1152], P(None, 'tensor', 'dp'), may hold values from -1.25 to 1.25
- proj_bias: float32 [1, 1152], replicated, may hold values from -3 to 3
- up_weight: bfloat16 [1, 1152, 4608], P(None, 'dp', 'tensor'), may hold values from -0.1875 to 0.1875
- up_bias: float32 [1, 4608], replicated, may hold values from -3 to 3
- down_weight: bfloat16 [1, 4608, 1152], P(None, 'tensor', 'dp'), may hold values from -0.125 to 0.125
- down_bias: float32 [1, 1152], replicated, may hold values from -3 to 3
- grad_output: float32 [4096, 1152], P(('dp', 'tensor')), may hold values from -6 to 6
Outputs:
- output: float32 [4096, 1152], P(('dp', 'tensor'))
- grad_tokens: float32 [4096, 1152], P(('dp', 'tensor'))
- grad_time_weight: float32 [256, 1152], P(None, 'dp')
- grad_class_table: float32 [1001, 1152], P(None, 'dp')
- grad_mod_weight: float32 [1, 1152, 6912], P(None, 'dp', 'tensor')
- grad_mod_bias: float32 [1, 6912], replicated
- grad_qkv_weight: float32 [1, 3, 1152, 1152], P(None, None, 'dp', 'tensor')
- grad_qv_bias: float32 [1, 2, 1152], replicated
- grad_proj_weight: float32 [1, 1152, 1152], P(None, 'tensor', 'dp')
- grad_proj_bias: float32 [1, 1152], replicated
- grad_up_weight: float32 [1, 1152, 4608], P(None, 'dp', 'tensor')
- grad_up_bias: float32 [1, 4608], replicated
- grad_down_weight: float32 [1, 4608, 1152], P(None, 'tensor', 'dp')
- grad_down_bias: float32 [1, 1152], replicated
All inputs are finite; a program needn't handle non-finite values.
Results may differ from a plain program's by a relative error of at most 0.025.
Values may be sent and summed in bfloat16 or wider, within the bound.
A program may use at most 128 MiB of HBM per device.

v0:
```python
import math
import jax
import jax.numpy as jnp
from jax import lax
from jax.sharding import PartitionSpec as P

HEAD_DIM = 72
SEQ = 256
LAYERS = 1
EPSILON = 1e-06
PRECISE = lax.Precision.HIGHEST
GELU_COEFF = math.sqrt(2.0 / math.pi)
CUBIC_COEFF = 0.044715


def time_features(timesteps, width):
    half_width = width // 2
    freq_rates = jnp.exp(
        -math.log(10000.0) * jnp.arange(half_width, dtype=jnp.float32) / half_width
    )
    angles = timesteps.astype(jnp.float32)[:, None] * freq_rates[None, :]
    return jnp.concatenate([jnp.cos(angles), jnp.sin(angles)], axis=1)


def layer_norm(values):
    average = jnp.mean(values, axis=-1, keepdims=True)
    centred = values - average
    inverse = lax.rsqrt(jnp.mean(centred * centred, axis=-1, keepdims=True) + EPSILON)
    return (centred * inverse, inverse)


def norm_back(normed, inverse, grad_normed):
    first = jnp.mean(grad_normed, axis=-1, keepdims=True)
    second = jnp.mean(grad_normed * normed, axis=-1, keepdims=True)
    return inverse * (grad_normed - first - normed * second)


def gelu_value(values):
    return (
        0.5
        * values
        * (1.0 + jnp.tanh(GELU_COEFF * (values + CUBIC_COEFF * values * values * values)))
    )


def gelu_slope(values):
    tangent = jnp.tanh(GELU_COEFF * (values + CUBIC_COEFF * values * values * values))
    return 0.5 * (1.0 + tangent) + 0.5 * values * (1.0 - tangent * tangent) * GELU_COEFF * (
        1.0 + 3.0 * CUBIC_COEFF * values * values
    )


def silu_slope(values):
    logistic = jax.nn.sigmoid(values)
    return logistic * (1.0 + values * (1.0 - logistic))


def split_heads(values, latent_count):
    return values.reshape(latent_count, SEQ, -1, HEAD_DIM)


def local(
    tokens,
    timesteps,
    labels,
    time_weight,
    class_table,
    mod_weight,
    mod_bias,
    qkv_weight,
    qv_bias,
    proj_weight,
    proj_bias,
    up_weight,
    up_bias,
    down_weight,
    down_bias,
    grad_output,
):
    rows_own, model_width = tokens.shape
    tensor_count = lax.axis_size("tensor")
    tensor_place = lax.axis_index("tensor")
    group_rows = rows_own * tensor_count
    latent_count = group_rows // SEQ
    head_cols = qkv_weight.shape[3]
    unit_cols = up_weight.shape[2]
    mod_cols = mod_weight.shape[2]
    head_start = tensor_place * head_cols
    unit_start = tensor_place * unit_cols
    col_start = tensor_place * mod_cols
    score_scale = 1.0 / math.sqrt(HEAD_DIM)
    features = time_features(timesteps, time_weight.shape[0])
    one_hot = (
        labels[:, None] == jnp.arange(class_table.shape[0], dtype=jnp.int32)[None, :]
    ).astype(jnp.float32)
    condition = jnp.dot(features, time_weight, precision=PRECISE) + jnp.dot(
        one_hot, class_table, precision=PRECISE
    )
    cond_act = jax.nn.silu(condition).astype(jnp.bfloat16)
    mod_terms = jnp.stack([jnp.dot(cond_act, mod_weight[0], preferred_element_type=jnp.float32)])
    mod_own = lax.psum_scatter(mod_terms, "dp", scatter_dimension=1, tiled=True)
    mod_own = mod_own + lax.dynamic_slice_in_dim(mod_bias, col_start, mod_cols, 1)[:, None, :]
    modulation = lax.all_gather(mod_own, "tensor", axis=2, tiled=True)
    row_latent = (tensor_place * rows_own + jnp.arange(rows_own, dtype=jnp.int32)) // SEQ
    selector = (row_latent[:, None] == jnp.arange(latent_count, dtype=jnp.int32)[None, :]).astype(
        jnp.float32
    )

    def per_row(values):
        return jnp.dot(selector, values, precision=PRECISE)

    def per_latent(values):
        return jnp.dot(selector.T, values, precision=PRECISE)

    def mod_pieces(current):
        rows_mod = per_row(modulation[current])
        return [
            rows_mod[:, segment * model_width : (segment + 1) * model_width] for segment in range(6)
        ]

    def gather_layer(current):
        return (
            lax.all_gather(qkv_weight[current], "dp", axis=1, tiled=True),
            lax.all_gather(proj_weight[current], "dp", axis=1, tiled=True),
            lax.all_gather(up_weight[current], "dp", axis=0, tiled=True),
            lax.all_gather(down_weight[current], "dp", axis=1, tiled=True),
        )

    def spread_rows(values):
        return lax.all_gather(values, "tensor", axis=0, tiled=True)

    def sum_rows(values):
        return lax.psum_scatter(
            values.astype(jnp.bfloat16), "tensor", scatter_dimension=0, tiled=True
        ).astype(jnp.float32)

    def spread_grads(values):
        return lax.all_gather(values, "tensor", axis=0, tiled=True)

    def sum_grads(values):
        return lax.psum_scatter(
            values.astype(jnp.bfloat16), "tensor", scatter_dimension=0, tiled=True
        ).astype(jnp.float32)

    def attention_scores(queries, key_rows):
        return (
            jnp.einsum(
                "bqhd,bkhd->bhqk",
                split_heads(queries, latent_count),
                split_heads(key_rows, latent_count),
                preferred_element_type=jnp.float32,
            )
            * score_scale
        )

    kept_weights = []
    current_x = tokens
    current = 0
    layer_full = gather_layer(current)
    kept_weights.append(layer_full)
    qkv_full, proj_full, up_full, down_full = layer_full
    shift_attn, scale_attn, gate_attn, shift_mlp, scale_mlp, gate_mlp = mod_pieces(current)
    bias_query = lax.dynamic_slice_in_dim(qv_bias[current, 0], head_start, head_cols, 0)
    bias_value = lax.dynamic_slice_in_dim(qv_bias[current, 1], head_start, head_cols, 0)
    unit_bias = lax.dynamic_slice_in_dim(up_bias[current], unit_start, unit_cols, 0)
    normed_attn, inverse_attn = layer_norm(current_x)
    attn_in = spread_rows((normed_attn * (1.0 + scale_attn) + shift_attn).astype(jnp.bfloat16))
    queries = (
        jnp.dot(attn_in, qkv_full[0], preferred_element_type=jnp.float32) + bias_query
    ).astype(jnp.bfloat16)
    key_rows = jnp.dot(attn_in, qkv_full[1], preferred_element_type=jnp.float32).astype(
        jnp.bfloat16
    )
    value_rows = (
        jnp.dot(attn_in, qkv_full[2], preferred_element_type=jnp.float32) + bias_value
    ).astype(jnp.bfloat16)
    scores = attention_scores(queries, key_rows)
    log_total = jnp.log(jnp.sum(jnp.exp(scores), axis=-1, keepdims=True))
    prob_low = jnp.exp(scores - log_total).astype(jnp.bfloat16)
    attended = (
        jnp.einsum(
            "bhqk,bkhd->bqhd",
            prob_low,
            split_heads(value_rows, latent_count),
            preferred_element_type=jnp.float32,
        )
        .astype(jnp.bfloat16)
        .reshape(group_rows, head_cols)
    )
    attn_out = (
        sum_rows(jnp.dot(attended, proj_full, preferred_element_type=jnp.float32))
        + proj_bias[current]
    )
    middle = current_x + gate_attn * attn_out
    normed_mlp, inverse_mlp = layer_norm(middle)
    mlp_in = spread_rows((normed_mlp * (1.0 + scale_mlp) + shift_mlp).astype(jnp.bfloat16))
    pre_act = jnp.dot(mlp_in, up_full, preferred_element_type=jnp.float32) + unit_bias
    gelu_low = gelu_value(pre_act).astype(jnp.bfloat16)
    mlp_out = (
        sum_rows(jnp.dot(gelu_low, down_full, preferred_element_type=jnp.float32))
        + down_bias[current]
    )
    stored = [
        (
            normed_attn,
            inverse_attn,
            attn_in,
            queries,
            key_rows,
            value_rows,
            log_total,
            attended,
            attn_out,
            normed_mlp,
            inverse_mlp,
            mlp_in,
            pre_act,
            gelu_low,
            mlp_out,
        )
    ]
    current_x = middle + gate_mlp * mlp_out
    grad_x = grad_output
    mod_list = [None] * LAYERS
    qkv_list = [None] * LAYERS
    proj_list = [None] * LAYERS
    up_list = [None] * LAYERS
    down_list = [None] * LAYERS
    qv_bias_list = [None] * LAYERS
    proj_bias_list = [None] * LAYERS
    unit_bias_list = [None] * LAYERS
    down_bias_list = [None] * LAYERS
    for current in reversed(range(LAYERS)):
        (
            normed_attn,
            inverse_attn,
            attn_in,
            queries,
            key_rows,
            value_rows,
            log_total,
            attended,
            attn_out,
            normed_mlp,
            inverse_mlp,
            mlp_in,
            pre_act,
            gelu_low,
            mlp_out,
        ) = stored[current]
        qkv_full, proj_full, up_full, down_full = gather_layer(current)
        shift_attn, scale_attn, gate_attn, shift_mlp, scale_mlp, gate_mlp = mod_pieces(current)
        d_mlp = grad_x * gate_mlp
        d_gate_mlp = per_latent(grad_x * mlp_out)
        down_bias_list[current] = jnp.sum(d_mlp, axis=0)
        d_mlp_all = spread_grads(d_mlp.astype(jnp.bfloat16))
        grad_down = jnp.dot(gelu_low.T, d_mlp_all, preferred_element_type=jnp.float32)
        d_gelu = jnp.dot(d_mlp_all, down_full.T, preferred_element_type=jnp.float32)
        d_pre = d_gelu * gelu_slope(pre_act)
        unit_part = jnp.sum(d_pre, axis=0)
        unit_bias_list[current] = lax.dynamic_update_slice_in_dim(
            jnp.zeros((up_bias.shape[1],), jnp.float32), unit_part, unit_start, 0
        )
        d_pre_low = d_pre.astype(jnp.bfloat16)
        grad_up = jnp.dot(mlp_in.T, d_pre_low, preferred_element_type=jnp.float32)
        d_mlp_in = sum_grads(jnp.dot(d_pre_low, up_full.T, preferred_element_type=jnp.float32))
        d_shift_mlp = per_latent(d_mlp_in)
        d_scale_mlp = per_latent(d_mlp_in * normed_mlp)
        d_middle = grad_x + norm_back(normed_mlp, inverse_mlp, d_mlp_in * (1.0 + scale_mlp))
        d_attn = d_middle * gate_attn
        d_gate_attn = per_latent(d_middle * attn_out)
        proj_bias_list[current] = jnp.sum(d_attn, axis=0)
        d_attn_all = spread_grads(d_attn.astype(jnp.bfloat16))
        grad_proj = jnp.dot(attended.T, d_attn_all, preferred_element_type=jnp.float32)
        d_attended = jnp.dot(d_attn_all, proj_full.T, preferred_element_type=jnp.float32).astype(
            jnp.bfloat16
        )
        scores = attention_scores(queries, key_rows)
        prob_full = jnp.exp(scores - log_total)
        prob_low = prob_full.astype(jnp.bfloat16)
        d_heads = split_heads(d_attended, latent_count)
        grad_value = jnp.einsum(
            "bhqk,bqhd->bkhd", prob_low, d_heads, preferred_element_type=jnp.float32
        ).reshape(group_rows, head_cols)
        d_prob = jnp.einsum(
            "bqhd,bkhd->bhqk",
            d_heads,
            split_heads(value_rows, latent_count),
            preferred_element_type=jnp.float32,
        )
        row_delta = jnp.einsum(
            "bqhd,bqhd->bhq",
            d_heads,
            split_heads(attended, latent_count),
            preferred_element_type=jnp.float32,
        )
        d_scores = prob_full * (d_prob - row_delta[..., None])
        d_score_low = d_scores.astype(jnp.bfloat16)
        grad_query = (
            jnp.einsum(
                "bhqk,bkhd->bqhd",
                d_score_low,
                split_heads(key_rows, latent_count),
                preferred_element_type=jnp.float32,
            ).reshape(group_rows, head_cols)
            * score_scale
        )
        grad_key = (
            jnp.einsum(
                "bhqk,bqhd->bkhd",
                d_score_low,
                split_heads(queries, latent_count),
                preferred_element_type=jnp.float32,
            ).reshape(group_rows, head_cols)
            * score_scale
        )
        qv_part = jnp.stack([jnp.sum(grad_query, axis=0), jnp.sum(grad_value, axis=0)])
        qv_bias_list[current] = lax.dynamic_update_slice_in_dim(
            jnp.zeros((2, model_width), jnp.float32), qv_part, head_start, 1
        )
        query_low = grad_query.astype(jnp.bfloat16)
        key_low = grad_key.astype(jnp.bfloat16)
        value_low = grad_value.astype(jnp.bfloat16)
        grad_qkv = jnp.stack(
            [
                jnp.dot(attn_in.T, query_low, preferred_element_type=jnp.float32),
                jnp.dot(attn_in.T, key_low, preferred_element_type=jnp.float32),
                jnp.dot(attn_in.T, value_low, preferred_element_type=jnp.float32),
            ]
        )
        d_attn_terms = (
            jnp.dot(query_low, qkv_full[0].T, preferred_element_type=jnp.float32)
            + jnp.dot(key_low, qkv_full[1].T, preferred_element_type=jnp.float32)
            + jnp.dot(value_low, qkv_full[2].T, preferred_element_type=jnp.float32)
        )
        d_attn_in = sum_grads(d_attn_terms)
        d_shift_attn = per_latent(d_attn_in)
        d_scale_attn = per_latent(d_attn_in * normed_attn)
        grad_x = d_middle + norm_back(normed_attn, inverse_attn, d_attn_in * (1.0 + scale_attn))
        mod_list[current] = jnp.concatenate(
            [d_shift_attn, d_scale_attn, d_gate_attn, d_shift_mlp, d_scale_mlp, d_gate_mlp], axis=1
        )
        qkv_list[current], proj_list[current], up_list[current], down_list[current] = (
            lax.psum_scatter(
                grad_qkv.astype(jnp.bfloat16), "dp", scatter_dimension=1, tiled=True
            ).astype(jnp.float32),
            lax.psum_scatter(
                grad_proj.astype(jnp.bfloat16), "dp", scatter_dimension=1, tiled=True
            ).astype(jnp.float32),
            lax.psum_scatter(
                grad_up.astype(jnp.bfloat16), "dp", scatter_dimension=0, tiled=True
            ).astype(jnp.float32),
            lax.psum_scatter(
                grad_down.astype(jnp.bfloat16), "dp", scatter_dimension=1, tiled=True
            ).astype(jnp.float32),
        )
    d_mod_part = jnp.stack(mod_list)
    qv_total, proj_total, unit_total, down_total, modb_total = lax.psum(
        (
            jnp.stack(qv_bias_list),
            jnp.stack(proj_bias_list),
            jnp.stack(unit_bias_list),
            jnp.stack(down_bias_list),
            jnp.sum(d_mod_part, axis=1),
        ),
        ("dp", "tensor"),
    )
    d_mod = lax.psum(d_mod_part.astype(jnp.bfloat16), "tensor").astype(jnp.float32)
    d_mod_all = lax.all_gather(
        lax.dynamic_slice_in_dim(d_mod, col_start, mod_cols, 2), "dp", axis=1, tiled=True
    )
    cond_wide = cond_act.astype(jnp.float32)
    grad_mod_weight = jnp.stack([jnp.dot(cond_wide.T, d_mod_all[0], precision=PRECISE)])
    cond_back = jnp.dot(d_mod_all[0], mod_weight[0].astype(jnp.float32).T, precision=PRECISE)
    d_cond_act = lax.psum(cond_back, "tensor")
    d_condition = d_cond_act * silu_slope(condition)
    grad_time_weight = jnp.dot(features.T, d_condition, precision=PRECISE)
    grad_class_table = jnp.dot(one_hot.T, d_condition, precision=PRECISE)
    return (
        current_x,
        grad_x,
        grad_time_weight,
        grad_class_table,
        grad_mod_weight,
        modb_total,
        jnp.stack(qkv_list),
        qv_total,
        jnp.stack(proj_list),
        proj_total,
        jnp.stack(up_list),
        unit_total,
        jnp.stack(down_list),
        down_total,
    )


def solution(mesh):
    in_specs = (
        P(("dp", "tensor"), None),
        P(),
        P(),
        P(None, "dp"),
        P(None, "dp"),
        P(None, "dp", "tensor"),
        P(),
        P(None, None, "dp", "tensor"),
        P(),
        P(None, "tensor", "dp"),
        P(),
        P(None, "dp", "tensor"),
        P(),
        P(None, "tensor", "dp"),
        P(),
        P(("dp", "tensor"), None),
    )
    out_specs = (
        P(("dp", "tensor"), None),
        P(("dp", "tensor"), None),
        P(None, "dp"),
        P(None, "dp"),
        P(None, "dp", "tensor"),
        P(),
        P(None, None, "dp", "tensor"),
        P(),
        P(None, "tensor", "dp"),
        P(),
        P(None, "dp", "tensor"),
        P(),
        P(None, "tensor", "dp"),
        P(),
    )
    return jax.shard_map(local, mesh=mesh, in_specs=in_specs, out_specs=out_specs, check_vma=False)
```

profile of v0, /device:TPU:0, one launch (start us, length us, event | category | flops | bytes accessed | tf_op | source)
XLA Modules:
  0.0 829.4 jit_solution(17721218927461385044)
XLA Ops:
  10.7 1.9 convolution_bitcast_fusion.1
  16.1 69.0 %all-reduce.4.cloned.1.call-done = f32[1,16,1728]{2,1,0:T(8,128)} async-done(((f32[1,16,1728]{2,1,0:T(8,128)}), f32[1,16,1728]{2,1,0:T(8,128)}) %all-reduce.4.cloned.1.call-update) | async-done | bytes 110608
  87.2 23.5 %all_gather.34 = f32[1,2,6912]{1,0,2:T(1,128)S(1)} all-gather(f32[1,2,1728]{1,0,2:T(1,128)S(1)} %copy.63), channel_id=1, replica_groups=mesh['dp'=8,'tensor'=4] {'tensor'}, dimensions={2}, use_global_device_ids=true | all-gather | bytes 69120 | tf_op jit(solution)/shard_map/all_gather | solution.py:103
  110.8 2.2 fusion.79
  116.6 35.3 %all-gather.1 = bf16[1,288,1152]{1,2,0:T(8,128)(2,1)} all-gather(bf16[1,288,144]{1,2,0:T(8,128)(2,1)S(1)} %copy-done.24), channel_id=3, replica_groups=mesh['dp'=8,'tensor'=4] {'dp'}, dimensions={2}, use_global_device_ids=true | all-gather | bytes 746496 | tf_op jit(solution)/shard_map/all_gather | solution.py:124
  151.9 38.0 %all-gather.20.cloned.1.call-done = bf16[1,3,1152,288]{3,2,1,0:T(8,128)(2,1)} async-done(((bf16[1,3,144,288]{3,2,1,0:T(8,128)(2,1)}), bf16[1,3,1152,288]{3,2,1,0:T(8,128)(2,1)}) %all-gather.20.cloned.1.call-update) | async-done | bytes 1990672 | tf_op jit(solution)/shard_map/all_gather | solution.py:123
  189.9 2.1 fusion.21
  192.1 1.9 convolution_convert_fusion.10
  194.1 1.9 fusion.20
  196.1 1.9 fusion.61
  197.9 3.0 convolution_convert_fusion.11
  202.1 3.0 convolution_convert_fusion.4
  205.9 23.6 %reduce-scatter.12.cloned.1.call-done = bf16[128,1152]{1,0:T(8,128)(2,1)} async-done(((bf16[512,1152]{1,0:T(8,128)(2,1)}), bf16[128,1152]{1,0:T(8,128)(2,1)}) %reduce-scatter.12.cloned.1.call-update) | async-done | bytes 294928 | tf_op jit(solution)/shard_map/reduce_scatter | solution.py:133
  231.1 2.4 fusion.68
  236.2 50.3 %all-gather.22.cloned.1.call-done = bf16[1,1152,1152]{2,1,0:T(8,128)(2,1)} async-done(((bf16[1,144,1152]{2,1,0:T(8,128)(2,1)}), bf16[1,1152,1152]{2,1,0:T(8,128)(2,1)}) %all-gather.22.cloned.1.call-update) | async-done | bytes 2654224 | tf_op jit(solution)/shard_map/all_gather | solution.py:125
  286.5 18.0 %all-gather.14.cloned.1.call-done = bf16[512,1152]{1,0:T(8,128)(2,1)} async-done(((bf16[128,1152]{1,0:T(8,128)(2,1)}), bf16[512,1152]{1,0:T(8,128)(2,1)}) %all-gather.14.cloned.1.call-update) | async-done | bytes 1179664 | tf_op jit(solution)/shard_map/all_gather | solution.py:130
  304.5 5.4 convolution_add_fusion.2
  309.9 51.8 %all-gather.24.cloned.1.call-done = bf16[1,1152,1152]{1,2,0:T(8,128)(2,1)} async-done(((bf16[1,1152,144]{1,2,0:T(8,128)(2,1)}), bf16[1,1152,1152]{1,2,0:T(8,128)(2,1)}) %all-gather.24.cloned.1.call-update) | async-done | bytes 2654224 | tf_op jit(solution)/shard_map/all_gather | solution.py:126
  361.7 18.2 %all-gather.16.cloned.1.call-done = bf16[512,1152]{1,0:T(8,128)(2,1)} async-done(((bf16[128,1152]{1,0:T(8,128)(2,1)}), bf16[512,1152]{1,0:T(8,128)(2,1)}) %all-gather.16.cloned.1.call-update) | async-done | bytes 1179664 | tf_op jit(solution)/shard_map/all_gather | solution.py:138
  379.9 6.0 fusion.104
  386.9 2.9 convolution_convert_fusion.2
  389.9 5.7 convolution_convert_fusion.3
  396.3 19.3 %reduce-scatter.16.cloned.1.call-done = bf16[128,1152]{1,0:T(8,128)(2,1)} async-done(((bf16[512,1152]{1,0:T(8,128)(2,1)}), bf16[128,1152]{1,0:T(8,128)(2,1)}) %reduce-scatter.16.cloned.1.call-update) | async-done | bytes 294928 | tf_op jit(solution)/shard_map/reduce_scatter | solution.py:141
  418.1 25.6 %reduce-scatter.14.cloned.1.call-done = bf16[128,1152]{1,0:T(8,128)(2,1)} async-done(((bf16[512,1152]{1,0:T(8,128)(2,1)}), bf16[128,1152]{1,0:T(8,128)(2,1)}) %reduce-scatter.14.cloned.1.call-update) | async-done | bytes 294928 | tf_op jit(solution)/shard_map/reduce_scatter | solution.py:133
  443.7 2.7 fusion.66
  446.5 4.9 convolution_convert_fusion.1
  451.5 5.4 convolution_convert_fusion
  457.2 4.2 fusion.14
  461.4 2.7 all-gather.18.cloned.1.call-done
  464.0 2.8 convolution_convert_fusion.9
  470.9 2.3 multiply_convert_fusion.1
  476.0 1.8 convolution_convert_fusion.5
  477.9 4.5 fusion.100
  485.3 1.8 convert_bitcast_fusion
  489.2 1.9 fusion.1
  498.4 7.2 copy.97
  505.6 7.5 reshape.264
  513.6 25.8 %reduce-scatter.22.cloned.1.call-done = bf16[144,1152]{1,0:T(8,128)(2,1)} async-done(((bf16[1152,1152]{1,0:T(8,128)(2,1)}), bf16[144,1152]{1,0:T(8,128)(2,1)}) %reduce-scatter.22.cloned.1.call-update) | async-done | bytes 331792 | tf_op jit(solution)/shard_map/reduce_scatter | solution.py:350
  539.3 1.9 bitcast_convert_fusion.3
  541.2 72.6 %reduce-scatter.24.cloned.1.call-done = bf16[1152,144]{0,1:T(8,128)(2,1)} async-done(((bf16[1152,1152]{0,1:T(8,128)(2,1)}), bf16[1152,144]{0,1:T(8,128)(2,1)}) %reduce-scatter.24.cloned.1.call-update) | async-done | bytes 331792 | tf_op jit(solution)/shard_map/reduce_scatter | solution.py:353
  613.8 1.9 bitcast_convert_fusion.2
  615.7 63.0 %reduce-scatter.20.cloned.1.call-done = bf16[288,144]{0,1:T(8,128)(2,1)} async-done(((bf16[288,1152]{0,1:T(8,128)(2,1)}), bf16[288,144]{0,1:T(8,128)(2,1)}) %reduce-scatter.20.cloned.1.call-update) | async-done | bytes 82960 | tf_op jit(solution)/shard_map/reduce_scatter | solution.py:347
  680.3 25.2 %reduce-scatter.18.cloned.1.call-done = bf16[128,1152]{1,0:T(8,128)(2,1)} async-done(((bf16[512,1152]{1,0:T(8,128)(2,1)}), bf16[128,1152]{1,0:T(8,128)(2,1)}) %reduce-scatter.18.cloned.1.call-update) | async-done | bytes 294928 | tf_op jit(solution)/shard_map/reduce_scatter | solution.py:141
  719.6 10.7 %psum.49 = bf16[1,2,6912]{2,1,0:T(2,128)(2,1)S(1)} all-reduce(bf16[1,2,6912]{2,1,0:T(2,128)(2,1)S(1)} %copy-done.35), channel_id=1, replica_groups=mesh['dp'=8,'tensor'=4] {'tensor'}, use_global_device_ids=true, to_apply=%region_14.15 | all-reduce | flops 13824 | bytes 55296 | tf_op jit(solution)/shard_map/psum | solution.py:368
  730.4 31.0 %all_gather.43 = f32[1,16,1728]{2,0,1:T(1,128)S(1)} all-gather(f32[1,2,1728]{2,0,1:T(1,128)S(1)} %copy.81), channel_id=1, replica_groups=mesh['dp'=8,'tensor'=4] {'dp'}, dimensions={1}, use_global_device_ids=true | all-gather | bytes 124416 | tf_op jit(solution)/shard_map/all_gather | solution.py:369
  761.9 11.0 %psum.50 = f32[16,144]{1,0:T(8,128)S(1)} all-reduce(f32[16,144]{1,0:T(8,128)S(1)} %fusion.39), channel_id=1, replica_groups=mesh['dp'=8,'tensor'=4] {'tensor'}, use_global_device_ids=true, to_apply=%region_15.16 | all-reduce | flops 2304 | bytes 18432 | tf_op jit(solution)/shard_map/psum | solution.py:375
  772.9 40.4 %all-reduce.1 = (f32[1,6912]{1,0:T(1,128)}, f32[1,2,1152]{2,1,0:T(2,128)}, f32[1,1152]{1,0:T(1,128)}, f32[1,4608]{1,0:T(1,128)}, f32[1,1152]{1,0:T(1,128)}) all-reduce(f32[1,6912]{1,0:T(1,128)S(1)} %reduce_sum.147, f32[1,2,1152]{2,1,0:T(2,128)S(1)} %copy-done.33, ...), channel_id=1, replica_groups=mesh['dp'=8,'tensor'=4] {'dp','tensor'}, use_global_device_ids=true, to_apply=%region_17.18 | all-reduce | flops 16128 | bytes 129024 | tf_op jit(solution)/shard_map/psum | solution.py:358
  817.2 2.2 multiply_add_fusion.1
  (226 shorter events, 65.2 us)
Async XLA Ops:
  7.2 7.7 copy-start.50
  7.2 6.6 copy-start.3
  7.2 77.9 %all-reduce.4.cloned.1.call-start = ((), (), s32[]{:S(2)}) async-start(), calls=%async_computation.23 | async-start | bytes 229376
  8.4 76.7 %copy-start.26 = (f32[16,128]{1,0:T(8,128)}, f32[16,128]{1,0:T(8,128)S(1)}, u32[]{:S(2)}) copy-start(f32[16,128]{1,0:T(8,128)S(1)} %get-tuple-element.82) | copy-start | bytes 24580
  8.4 76.7 %copy-start.28 = (f32[16,128]{1,0:T(8,128)}, f32[16,128]{1,0:T(8,128)S(1)}, u32[]{:S(2)}) copy-start(f32[16,128]{1,0:T(8,128)S(1)} %get-tuple-element.83) | copy-start | bytes 24580
  12.6 139.3 %all-gather.12.cloned.1.call-start = ((), (), s32[]{:S(2)}) async-start(), calls=%async_computation.8 | async-start | bytes 1474560 | tf_op jit(solution)/shard_map/all_gather | solution.py:130
  13.8 99.2 %copy-start.37 = (f32[128]{0:T(128)}, f32[128]{0:T(128)S(1)}, u32[]{:S(2)}) copy-start(f32[128]{0:T(128)S(1)} %broadcast_multiply_fusion.5) | copy-start | bytes 1540
  14.0 99.0 %copy-start.41 = (f32[128]{0:T(128)}, f32[128]{0:T(128)S(1)}, u32[]{:S(2)}) copy-start(f32[128]{0:T(128)S(1)} %add_rsqrt_fusion.1) | copy-start | bytes 1540
  16.1 94.6 %copy-start.36 = (s32[128]{0:T(128)}, s32[128]{0:T(128)S(1)}, u32[]{:S(2)}) copy-start(s32[128]{0:T(128)S(1)} %and_select_fusion) | copy-start | bytes 1540
  115.7 74.2 %all-gather.20.cloned.1.call-start = ((), (), s32[]{:S(2)}) async-start(), calls=%async_computation.19 | async-start | bytes 2985984 | tf_op jit(solution)/shard_map/all_gather | solution.py:123
  116.5 113.0 %reduce-scatter.12.cloned.1.call-start = ((), (), s32[]{:S(2)}) async-start(), calls=%async_computation.9 | async-start | bytes 1474560 | tf_op jit(solution)/shard_map/reduce_scatter | solution.py:133
  151.9 40.2 %copy-start.4 = (bf16[512,1152]{1,0:T(8,128)(2,1)S(1)}, bf16[512,1152]{1,0:T(8,128)(2,1)}, u32[]{:S(2)}) copy-start(bf16[512,1152]{1,0:T(8,128)(2,1)} %all-gather.12.cloned.1.call-done) | copy-start | bytes 3538948
  196.1 4.9 copy-start.21
  205.2 25.9 %copy-start.5 = (f32[128,1152]{1,0:T(8,128)S(1)}, f32[128,1152]{1,0:T(8,128)}, u32[]{:S(2)}) copy-start(f32[128,1152]{1,0:T(8,128)} %param.31) | copy-start | bytes 1769476
  205.2 81.3 %all-gather.22.cloned.1.call-start = ((), (), s32[]{:S(2)}) async-start(), calls=%async_computation.20 | async-start | bytes 2985984 | tf_op jit(solution)/shard_map/all_gather | solution.py:125
  205.8 98.8 %all-gather.14.cloned.1.call-start = ((), (), s32[]{:S(2)}) async-start(), calls=%async_computation.10 | async-start | bytes 1474560 | tf_op jit(solution)/shard_map/all_gather | solution.py:130
  205.9 27.6 %copy-start.25 = (f32[1152]{0:T(1024)}, f32[1152]{0:T(1024)S(1)}, u32[]{:S(2)}) copy-start(f32[1152]{0:T(1024)S(1)} %reduce.8) | copy-start | bytes 13828
  230.8 184.8 %copy-start.39 = (f32[128]{0:T(128)}, f32[128]{0:T(128)S(1)}, u32[]{:S(2)}) copy-start(f32[128]{0:T(128)S(1)} %broadcast_multiply_fusion.4) | copy-start | bytes 1540
  231.0 184.6 %copy-start.43 = (f32[128]{0:T(128)}, f32[128]{0:T(128)S(1)}, u32[]{:S(2)}) copy-start(f32[128]{0:T(128)S(1)} %add_rsqrt_fusion) | copy-start | bytes 1540
  233.5 128.2 %all-gather.24.cloned.1.call-start = ((), (), s32[]{:S(2)}) async-start(), calls=%async_computation.21 | async-start | bytes 2985984 | tf_op jit(solution)/shard_map/all_gather | solution.py:126
  234.3 145.6 %all-gather.16.cloned.1.call-start = ((), (), s32[]{:S(2)}) async-start(), calls=%async_computation.12 | async-start | bytes 1474560 | tf_op jit(solution)/shard_map/all_gather | solution.py:138
  235.0 180.6 %reduce-scatter.16.cloned.1.call-start = ((), (), s32[]{:S(2)}) async-start(), calls=%async_computation.13 | async-start | bytes 1474560 | tf_op jit(solution)/shard_map/reduce_scatter | solution.py:141
  379.9 7.0 copy-start.49
  389.9 5.8 copy-start.46
  389.9 53.8 %reduce-scatter.14.cloned.1.call-start = ((), (), s32[]{:S(2)}) async-start(), calls=%async_computation.11 | async-start | bytes 1474560 | tf_op jit(solution)/shard_map/reduce_scatter | solution.py:133
  395.7 68.4 %all-gather.18.cloned.1.call-start = ((), (), s32[]{:S(2)}) async-start(), calls=%async_computation.14 | async-start | bytes 1474560 | tf_op jit(solution)/shard_map/all_gather | solution.py:138
  446.5 92.9 %reduce-scatter.22.cloned.1.call-start = ((), (), s32[]{:S(2)}) async-start(), calls=%async_computation.17 | async-start | bytes 2985984 | tf_op jit(solution)/shard_map/reduce_scatter | solution.py:350
  451.4 162.4 %reduce-scatter.24.cloned.1.call-start = ((), (), s32[]{:S(2)}) async-start(), calls=%async_computation.18 | async-start | bytes 2985984 | tf_op jit(solution)/shard_map/reduce_scatter | solution.py:353
  457.0 221.7 %reduce-scatter.20.cloned.1.call-start = ((), (), s32[]{:S(2)}) async-start(), calls=%async_computation.16 | async-start | bytes 995328 | tf_op jit(solution)/shard_map/reduce_scatter | solution.py:347
  477.8 227.7 %reduce-scatter.18.cloned.1.call-start = ((), (), s32[]{:S(2)}) async-start(), calls=%async_computation.15 | async-start | bytes 1474560 | tf_op jit(solution)/shard_map/reduce_scatter | solution.py:141
  482.3 5.1 copy-start.15
  491.2 328.2 %reduce-scatter.26.cloned.1.call-start = ((), (), s32[]{:S(2)}) async-start(), calls=%async_computation.22 | async-start | bytes 2322432
  505.6 7.5 copy-start.47
  505.6 7.6 copy-start.44
  513.3 196.2 %copy-start.17 = (bf16[128,1152]{1,0:T(8,128)(2,1)S(1)}, bf16[128,1152]{1,0:T(8,128)(2,1)}, u32[]{:S(2)}) copy-start(bf16[128,1152]{1,0:T(8,128)(2,1)} %reduce-scatter.12.cloned.1.call-done) | copy-start | bytes 884740
  513.3 197.9 %copy-start.10 = (bf16[128,1152]{1,0:T(8,128)(2,1)S(1)}, bf16[128,1152]{1,0:T(8,128)(2,1)}, u32[]{:S(2)}) copy-start(bf16[128,1152]{1,0:T(8,128)(2,1)} %reduce-scatter.16.cloned.1.call-done) | copy-start | bytes 884740
  513.5 166.7 %copy-start.32 = (f32[1,2,1152]{2,1,0:T(2,128)}, f32[1,2,1152]{2,1,0:T(2,128)S(1)}, u32[]{:S(2)}) copy-start(f32[1,2,1152]{2,1,0:T(2,128)S(1)} %dynamic_update_slice.8) | copy-start | bytes 27652
  541.2 173.3 %copy-start.18 = (bf16[128,1152]{1,0:T(8,128)(2,1)S(1)}, bf16[128,1152]{1,0:T(8,128)(2,1)}, u32[]{:S(2)}) copy-start(bf16[128,1152]{1,0:T(8,128)(2,1)} %reduce-scatter.14.cloned.1.call-done) | copy-start | bytes 884740
  705.5 12.3 %copy-start.6 = (bf16[128,1152]{1,0:T(8,128)(2,1)S(1)}, bf16[128,1152]{1,0:T(8,128)(2,1)}, u32[]{:S(2)}) copy-start(bf16[128,1152]{1,0:T(8,128)(2,1)} %reduce-scatter.18.cloned.1.call-done) | copy-start | bytes 884740
  715.6 45.8 %copy-start.16 = (bf16[1,144,1728]{2,1,0:T(8,128)(2,1)S(1)}, bf16[1,144,1728]{2,1,0:T(8,128)(2,1)}, u32[]{:S(2)}) copy-start(bf16[1,144,1728]{2,1,0:T(8,128)(2,1)} %param.21) | copy-start | bytes 1492996
  717.8 55.1 %copy-start.31 = (f32[1,4608]{1,0:T(1,128)S(1)}, f32[1,4608]{1,0:T(1,128)}, u32[]{:S(2)}) copy-start(f32[1,4608]{1,0:T(1,128)} %copy-done.30) | copy-start | bytes 55300
  717.8 55.1 %copy-start.33 = (f32[1,2,1152]{2,1,0:T(2,128)S(1)}, f32[1,2,1152]{2,1,0:T(2,128)}, u32[]{:S(2)}) copy-start(f32[1,2,1152]{2,1,0:T(2,128)} %copy-done.32) | copy-start | bytes 27652
  717.8 97.1 %copy-start.27 = (f32[16,128]{1,0:T(8,128)S(1)}, f32[16,128]{1,0:T(8,128)}, u32[]{:S(2)}) copy-start(f32[16,128]{1,0:T(8,128)} %copy-done.26) | copy-start | bytes 24580
  717.8 97.1 %copy-start.29 = (f32[16,128]{1,0:T(8,128)S(1)}, f32[16,128]{1,0:T(8,128)}, u32[]{:S(2)}) copy-start(f32[16,128]{1,0:T(8,128)} %copy-done.28) | copy-start | bytes 24580
  717.8 98.1 %copy-start.48 = (s32[16]{0:T(128)S(1)}, s32[16]{0:T(128)}, u32[]{:S(2)}) copy-start(s32[16]{0:T(128)} %param.18) | copy-start | bytes 196
  719.6 97.7 %copy-start.38 = (f32[128]{0:T(128)S(1)}, f32[128]{0:T(128)}, u32[]{:S(2)}) copy-start(f32[128]{0:T(128)} %copy-done.37) | copy-start | bytes 1540
  719.6 97.7 %copy-start.42 = (f32[128]{0:T(128)S(1)}, f32[128]{0:T(128)}, u32[]{:S(2)}) copy-start(f32[128]{0:T(128)} %copy-done.41) | copy-start | bytes 1540
  817.2 5.4 copy-start.1
  (20 other events, 50.7 us)
Sparse Core Ops, SparseCore 0:
  12.7 72.4 all-reduce.3
  115.8 16.3 all-gather.11
  134.5 55.3 all-gather.19
  205.3 24.1 reduce-scatter.11
  231.5 54.9 all-gather.21
  288.5 15.9 all-gather.13
  306.7 54.9 all-gather.23
  363.9 15.9 all-gather.15
  390.0 25.6 reduce-scatter.15
  418.1 25.6 reduce-scatter.13
  446.6 17.4 all-gather.17
  467.6 71.7 reduce-scatter.21
  543.0 70.7 reduce-scatter.23
  617.6 60.9 reduce-scatter.19
  681.1 24.3 reduce-scatter.17
  708.9 68.0 reduce-scatter.25
where the time goes:
time: 838 us; the launch traced here: 829 us
  waiting for transfers between devices  506 us (60%)
  blocking collectives  152 us (18%)
  matrix products  82.3 us (10%)
  local copies, waits for them, and re-layouts  39.9 us (5%)
  other arithmetic  32.1 us (4%)
  between operations  15.7 us (2%)
    reduce_scatter x1, waiting for transfers between devices, local(): lax.psum_scatter(grad_down.astype(jnp.bfloat16), 'dp', scatter_dimension=...  72.6 us
    unnamed x18, waiting for transfers between devices  71.8 us
    reduce_scatter x1, waiting for transfers between devices, local(): lax.psum_scatter(grad_proj.astype(jnp.bfloat16), 'dp', scatter_dimension=...  63 us
    all_gather x1, waiting for transfers between devices, gather_layer(): lax.all_gather(down_weight[current], 'dp', axis=1, tiled=True)  51.8 us
    all_gather x1, waiting for transfers between devices, gather_layer(): lax.all_gather(up_weight[current], 'dp', axis=0, tiled=True)  50.3 us
    reduce_scatter x2, waiting for transfers between devices, sum_rows(): lax.psum_scatter(values.astype(jnp.bfloat16), 'tensor', scatter_dimension...  49.2 us
    reduce_scatter x2, waiting for transfers between devices, sum_grads(): lax.psum_scatter(values.astype(jnp.bfloat16), 'tensor', scatter_dimension...  44.5 us
    psum x1, blocking collectives, local(): lax.psum((jnp.stack(qv_bias_list), jnp.stack(proj_bias_list), jnp.stack(u...  40.4 us
  transfers between devices with their start and end apart: 16, of which 14 were waited for; matrix products, arithmetic and copies ran while one was open for 13% of the time, Pallas kernels for 0%

commit v1 on v0

--- a/solution.py
+++ b/solution.py
@@ -123,7 +123,10 @@
             lax.all_gather(qkv_weight[current], "dp", axis=1, tiled=True),
             lax.all_gather(proj_weight[current], "dp", axis=1, tiled=True),
             lax.all_gather(up_weight[current], "dp", axis=0, tiled=True),
-            lax.all_gather(down_weight[current], "dp", axis=1, tiled=True),
+            jnp.concatenate(
+                lax.all_to_all(jnp.stack([down_weight[current]] * lax.axis_size("dp")), "dp", 0, 0),
+                axis=1,
+            ),
         )
 
     def spread_rows(values):

time: 838 us -> 799 us (0.953)
  waiting for transfers between devices: 506 us -> 461 us
    all_gather x1 -> x0, waiting for transfers between devices: 51.8 us -> none  [gather_layer(): lax.all_gather(down_weight[current], 'dp', axis=1, tiled=True)]
    all_gather x1, waiting for transfers between devices: 50.3 us -> 68 us  [gather_layer(): lax.all_gather(up_weight[current], 'dp', axis=0, tiled=True)]
    unnamed x120 -> x122, local copies, waits for them, and re-layouts: 26.8 us -> 26.1 us
    unnamed x18 -> x17, waiting for transfers between devices: 71.8 us -> 71.1 us
  transfers between devices with their start and end apart: 16 -> 16, of which waited for: 14 -> 13; matrix products, arithmetic and copies ran while one was open for 13% -> 14% of each run, Pallas kernels for 0% -> 0%
where the time goes in v1:
time: 799 us; the launch traced here: 790 us
  waiting for transfers between devices  461 us (58%)
  blocking collectives  152 us (19%)
  matrix products  82.3 us (10%)
  local copies, waits for them, and re-layouts  40.9 us (5%)
  other arithmetic  32.2 us (4%)
  between operations  15.7 us (2%)
    reduce_scatter x1, waiting for transfers between devices, local(): lax.psum_scatter(grad_down.astype(jnp.bfloat16), 'dp', scatter_dimension=...  72.4 us
    unnamed x17, waiting for transfers between devices  71.1 us
    all_gather x1, waiting for transfers between devices, gather_layer(): lax.all_gather(up_weight[current], 'dp', axis=0, tiled=True)  68 us
    reduce_scatter x1, waiting for transfers between devices, local(): lax.psum_scatter(grad_proj.astype(jnp.bfloat16), 'dp', scatter_dimension=...  63.3 us
    reduce_scatter x2, waiting for transfers between devices, sum_grads(): lax.psum_scatter(values.astype(jnp.bfloat16), 'tensor', scatter_dimension...  44.5 us
    reduce_scatter x2, waiting for transfers between devices, sum_rows(): lax.psum_scatter(values.astype(jnp.bfloat16), 'tensor', scatter_dimension...  43.1 us
    psum x1, blocking collectives, local(): lax.psum((jnp.stack(qv_bias_list), jnp.stack(proj_bias_list), jnp.stack(u...  40.2 us
    all_gather x1, waiting for transfers between devices, gather_layer(): lax.all_gather(qkv_weight[current], 'dp', axis=1, tiled=True)  38 us
  transfers between devices with their start and end apart: 16, of which 13 were waited for; matrix products, arithmetic and copies ran while one was open for 14% of the time, Pallas kernels for 0%

profile of v1, /device:TPU:0, one launch (start us, length us, event | category | flops | bytes accessed | tf_op | source)
XLA Modules:
  0.0 790.3 jit_solution(16258642754266853082)
XLA Ops:
  10.7 1.9 convolution_bitcast_fusion.1
  16.1 69.0 %all-reduce.4.cloned.1.call-done = f32[1,16,1728]{2,1,0:T(8,128)} async-done(((f32[1,16,1728]{2,1,0:T(8,128)}), f32[1,16,1728]{2,1,0:T(8,128)}) %all-reduce.4.cloned.1.call-update) | async-done | bytes 110608
  87.2 23.5 %all_gather.30 = f32[1,2,6912]{1,0,2:T(1,128)S(1)} all-gather(f32[1,2,1728]{1,0,2:T(1,128)S(1)} %copy.64), channel_id=1, replica_groups=mesh['dp'=8,'tensor'=4] {'tensor'}, dimensions={2}, use_global_device_ids=true | all-gather | bytes 69120 | tf_op jit(solution)/shard_map/all_gather | solution.py:103
  110.8 2.2 fusion.77
  116.6 35.3 %all-gather.1 = bf16[1,288,1152]{1,2,0:T(8,128)(2,1)} all-gather(bf16[1,288,144]{1,2,0:T(8,128)(2,1)S(1)} %copy-done.25), channel_id=3, replica_groups=mesh['dp'=8,'tensor'=4] {'dp'}, dimensions={2}, use_global_device_ids=true | all-gather | bytes 746496 | tf_op jit(solution)/shard_map/all_gather | solution.py:124
  151.9 38.0 %all-gather.18.cloned.1.call-done = bf16[1,3,1152,288]{3,2,1,0:T(8,128)(2,1)} async-done(((bf16[1,3,144,288]{3,2,1,0:T(8,128)(2,1)}), bf16[1,3,1152,288]{3,2,1,0:T(8,128)(2,1)}) %all-gather.18.cloned.1.call-update) | async-done | bytes 1990672 | tf_op jit(solution)/shard_map/all_gather | solution.py:123
  189.9 2.1 fusion.19
  192.1 1.9 convolution_convert_fusion.10
  194.1 1.9 fusion.18
  196.1 1.8 fusion.59
  197.9 3.0 convolution_convert_fusion.11
  201.3 3.2 convolution_convert_fusion.4
  206.9 4.5 all-to-all-start
  211.6 17.3 %reduce-scatter.12.cloned.1.call-done = bf16[128,1152]{1,0:T(8,128)(2,1)} async-done(((bf16[512,1152]{1,0:T(8,128)(2,1)}), bf16[128,1152]{1,0:T(8,128)(2,1)}) %reduce-scatter.12.cloned.1.call-update) | async-done | bytes 294928 | tf_op jit(solution)/shard_map/reduce_scatter | solution.py:136
  230.4 2.4 fusion.66
  234.9 68.0 %all-gather.20.cloned.1.call-done = bf16[1,1152,1152]{2,1,0:T(8,128)(2,1)} async-done(((bf16[1,144,1152]{2,1,0:T(8,128)(2,1)}), bf16[1,1152,1152]{2,1,0:T(8,128)(2,1)}) %all-gather.20.cloned.1.call-update) | async-done | bytes 2654224 | tf_op jit(solution)/shard_map/all_gather | solution.py:125
  302.9 18.3 %all-gather.12.cloned.1.call-done = bf16[512,1152]{1,0:T(8,128)(2,1)} async-done(((bf16[128,1152]{1,0:T(8,128)(2,1)}), bf16[512,1152]{1,0:T(8,128)(2,1)}) %all-gather.12.cloned.1.call-update) | async-done | bytes 1179664 | tf_op jit(solution)/shard_map/all_gather | solution.py:133
  321.2 5.4 convolution_add_fusion.2
  326.6 14.2 %all-gather.14.cloned.1.call-done = bf16[512,1152]{1,0:T(8,128)(2,1)} async-done(((bf16[128,1152]{1,0:T(8,128)(2,1)}), bf16[512,1152]{1,0:T(8,128)(2,1)}) %all-gather.14.cloned.1.call-update) | async-done | bytes 1179664 | tf_op jit(solution)/shard_map/all_gather | solution.py:141
  340.8 6.0 fusion.102
  347.9 3.0 convolution_convert_fusion.2
  350.9 5.7 convolution_convert_fusion.3
  357.3 19.3 %reduce-scatter.16.cloned.1.call-done = bf16[128,1152]{1,0:T(8,128)(2,1)} async-done(((bf16[512,1152]{1,0:T(8,128)(2,1)}), bf16[128,1152]{1,0:T(8,128)(2,1)}) %reduce-scatter.16.cloned.1.call-update) | async-done | bytes 294928 | tf_op jit(solution)/shard_map/reduce_scatter | solution.py:144
  379.0 25.8 %reduce-scatter.14.cloned.1.call-done = bf16[128,1152]{1,0:T(8,128)(2,1)} async-done(((bf16[512,1152]{1,0:T(8,128)(2,1)}), bf16[128,1152]{1,0:T(8,128)(2,1)}) %reduce-scatter.14.cloned.1.call-update) | async-done | bytes 294928 | tf_op jit(solution)/shard_map/reduce_scatter | solution.py:136
  404.8 2.7 fusion.64
  407.6 4.9 convolution_convert_fusion.1
  412.6 5.4 convolution_convert_fusion
  418.3 4.2 fusion.12
  422.5 2.6 all-gather.16.cloned.1.call-done
  425.2 2.8 convolution_convert_fusion.9
  432.0 2.3 multiply_convert_fusion.1
  437.1 1.8 convolution_convert_fusion.5
  439.0 4.5 fusion.98
  446.4 1.8 convert_bitcast_fusion
  450.4 1.9 fusion.1
  459.5 7.2 copy.98
  466.7 7.5 reshape.274
  474.6 25.4 %reduce-scatter.22.cloned.1.call-done = bf16[144,1152]{1,0:T(8,128)(2,1)} async-done(((bf16[1152,1152]{1,0:T(8,128)(2,1)}), bf16[144,1152]{1,0:T(8,128)(2,1)}) %reduce-scatter.22.cloned.1.call-update) | async-done | bytes 331792 | tf_op jit(solution)/shard_map/reduce_scatter | solution.py:353
  500.1 1.9 bitcast_convert_fusion.3
  501.9 72.4 %reduce-scatter.24.cloned.1.call-done = bf16[1152,144]{0,1:T(8,128)(2,1)} async-done(((bf16[1152,1152]{0,1:T(8,128)(2,1)}), bf16[1152,144]{0,1:T(8,128)(2,1)}) %reduce-scatter.24.cloned.1.call-update) | async-done | bytes 331792 | tf_op jit(solution)/shard_map/reduce_scatter | solution.py:356
  574.4 1.9 bitcast_convert_fusion.2
  576.2 63.3 %reduce-scatter.20.cloned.1.call-done = bf16[288,144]{0,1:T(8,128)(2,1)} async-done(((bf16[288,1152]{0,1:T(8,128)(2,1)}), bf16[288,144]{0,1:T(8,128)(2,1)}) %reduce-scatter.20.cloned.1.call-update) | async-done | bytes 82960 | tf_op jit(solution)/shard_map/reduce_scatter | solution.py:350
  641.2 25.2 %reduce-scatter.18.cloned.1.call-done = bf16[128,1152]{1,0:T(8,128)(2,1)} async-done(((bf16[512,1152]{1,0:T(8,128)(2,1)}), bf16[128,1152]{1,0:T(8,128)(2,1)}) %reduce-scatter.18.cloned.1.call-update) | async-done | bytes 294928 | tf_op jit(solution)/shard_map/reduce_scatter | solution.py:144
  680.5 10.7 %psum.49 = bf16[1,2,6912]{2,1,0:T(2,128)(2,1)S(1)} all-reduce(bf16[1,2,6912]{2,1,0:T(2,128)(2,1)S(1)} %copy-done.36), channel_id=1, replica_groups=mesh['dp'=8,'tensor'=4] {'tensor'}, use_global_device_ids=true, to_apply=%region_14.15 | all-reduce | flops 13824 | bytes 55296 | tf_op jit(solution)/shard_map/psum | solution.py:371
  691.2 31.3 %all_gather.38 = f32[1,16,1728]{2,0,1:T(1,128)S(1)} all-gather(f32[1,2,1728]{2,0,1:T(1,128)S(1)} %copy.82), channel_id=1, replica_groups=mesh['dp'=8,'tensor'=4] {'dp'}, dimensions={1}, use_global_device_ids=true | all-gather | bytes 124416 | tf_op jit(solution)/shard_map/all_gather | solution.py:372
  723.0 11.0 %psum.50 = f32[16,144]{1,0:T(8,128)S(1)} all-reduce(f32[16,144]{1,0:T(8,128)S(1)} %fusion.37), channel_id=1, replica_groups=mesh['dp'=8,'tensor'=4] {'tensor'}, use_global_device_ids=true, to_apply=%region_15.16 | all-reduce | flops 2304 | bytes 18432 | tf_op jit(solution)/shard_map/psum | solution.py:378
  734.0 40.2 %all-reduce.1 = (f32[1,6912]{1,0:T(1,128)}, f32[1,2,1152]{2,1,0:T(2,128)}, f32[1,1152]{1,0:T(1,128)}, f32[1,4608]{1,0:T(1,128)}, f32[1,1152]{1,0:T(1,128)}) all-reduce(f32[1,6912]{1,0:T(1,128)S(1)} %reduce_sum.147, f32[1,2,1152]{2,1,0:T(2,128)S(1)} %copy-done.34, ...), channel_id=1, replica_groups=mesh['dp'=8,'tensor'=4] {'dp','tensor'}, use_global_device_ids=true, to_apply=%region_17.18 | all-reduce | flops 16128 | bytes 129024 | tf_op jit(solution)/shard_map/psum | solution.py:361
  778.1 2.2 multiply_add_fusion.1
  (228 shorter events, 65.5 us)
Async XLA Ops:
  7.2 7.7 copy-start.51
  7.2 6.6 copy-start.3
  7.2 77.9 %all-reduce.4.cloned.1.call-start = ((), (), s32[]{:S(2)}) async-start(), calls=%async_computation.23 | async-start | bytes 229376
  8.4 76.7 %copy-start.27 = (f32[16,128]{1,0:T(8,128)}, f32[16,128]{1,0:T(8,128)S(1)}, u32[]{:S(2)}) copy-start(f32[16,128]{1,0:T(8,128)S(1)} %get-tuple-element.82) | copy-start | bytes 24580
  8.4 76.7 %copy-start.29 = (f32[16,128]{1,0:T(8,128)}, f32[16,128]{1,0:T(8,128)S(1)}, u32[]{:S(2)}) copy-start(f32[16,128]{1,0:T(8,128)S(1)} %get-tuple-element.83) | copy-start | bytes 24580
  12.6 139.3 %all-gather.10.cloned.1.call-start = ((), (), s32[]{:S(2)}) async-start(), calls=%async_computation.9 | async-start | bytes 1474560 | tf_op jit(solution)/shard_map/all_gather | solution.py:133
  13.8 99.2 %copy-start.38 = (f32[128]{0:T(128)}, f32[128]{0:T(128)S(1)}, u32[]{:S(2)}) copy-start(f32[128]{0:T(128)S(1)} %broadcast_multiply_fusion.5) | copy-start | bytes 1540
  14.0 99.0 %copy-start.42 = (f32[128]{0:T(128)}, f32[128]{0:T(128)S(1)}, u32[]{:S(2)}) copy-start(f32[128]{0:T(128)S(1)} %add_rsqrt_fusion.1) | copy-start | bytes 1540
  16.1 94.6 %copy-start.37 = (s32[128]{0:T(128)}, s32[128]{0:T(128)S(1)}, u32[]{:S(2)}) copy-start(s32[128]{0:T(128)S(1)} %and_select_fusion) | copy-start | bytes 1540
  115.7 74.2 %all-gather.18.cloned.1.call-start = ((), (), s32[]{:S(2)}) async-start(), calls=%async_computation.20 | async-start | bytes 2985984 | tf_op jit(solution)/shard_map/all_gather | solution.py:123
  116.5 112.4 %reduce-scatter.12.cloned.1.call-start = ((), (), s32[]{:S(2)}) async-start(), calls=%async_computation.10 | async-start | bytes 1474560 | tf_op jit(solution)/shard_map/reduce_scatter | solution.py:136
  151.9 40.2 %copy-start.4 = (bf16[512,1152]{1,0:T(8,128)(2,1)S(1)}, bf16[512,1152]{1,0:T(8,128)(2,1)}, u32[]{:S(2)}) copy-start(bf16[512,1152]{1,0:T(8,128)(2,1)} %all-gather.10.cloned.1.call-done) | copy-start | bytes 3538948
  201.3 5.6 copy-start.19
  204.6 98.4 %all-gather.20.cloned.1.call-start = ((), (), s32[]{:S(2)}) async-start(), calls=%async_computation.21 | async-start | bytes 2985984 | tf_op jit(solution)/shard_map/all_gather | solution.py:125
  206.9 119.6 %all-to-all-start = ((bf16[8,1152,144]{1,2,0:T(8,128)(2,1)}), bf16[8,1152,144]{1,2,0:T(8,128)(2,1)}, u32[]{:S(2)}, u32[]{:S(2)}) async-start(bf16[8,1152,144]{1,2,0:T(8,128)(2,1)} %stack.73), calls=%async_computation.1 | async-start | bytes 5308416 | tf_op jit(solution)/shard_map/all_to_all | solution.py:127
  211.5 19.0 %copy-start.5 = (f32[128,1152]{1,0:T(8,128)S(1)}, f32[128,1152]{1,0:T(8,128)}, u32[]{:S(2)}) copy-start(f32[128,1152]{1,0:T(8,128)} %param.31) | copy-start | bytes 1769476
  211.5 109.7 %all-gather.12.cloned.1.call-start = ((), (), s32[]{:S(2)}) async-start(), calls=%async_computation.11 | async-start | bytes 1474560 | tf_op jit(solution)/shard_map/all_gather | solution.py:133
  211.6 21.3 %copy-start.26 = (f32[1152]{0:T(1024)}, f32[1152]{0:T(1024)S(1)}, u32[]{:S(2)}) copy-start(f32[1152]{0:T(1024)S(1)} %reduce.8) | copy-start | bytes 13828
  230.2 146.4 %copy-start.40 = (f32[128]{0:T(128)}, f32[128]{0:T(128)S(1)}, u32[]{:S(2)}) copy-start(f32[128]{0:T(128)S(1)} %broadcast_multiply_fusion.4) | copy-start | bytes 1540
  230.4 146.2 %copy-start.44 = (f32[128]{0:T(128)}, f32[128]{0:T(128)S(1)}, u32[]{:S(2)}) copy-start(f32[128]{0:T(128)S(1)} %add_rsqrt_fusion) | copy-start | bytes 1540
  232.9 107.9 %all-gather.14.cloned.1.call-start = ((), (), s32[]{:S(2)}) async-start(), calls=%async_computation.13 | async-start | bytes 1474560 | tf_op jit(solution)/shard_map/all_gather | solution.py:141
  233.7 142.9 %reduce-scatter.16.cloned.1.call-start = ((), (), s32[]{:S(2)}) async-start(), calls=%async_computation.14 | async-start | bytes 1474560 | tf_op jit(solution)/shard_map/reduce_scatter | solution.py:144
  340.8 7.1 copy-start.50
  350.9 5.8 copy-start.47
  350.9 54.0 %reduce-scatter.14.cloned.1.call-start = ((), (), s32[]{:S(2)}) async-start(), calls=%async_computation.12 | async-start | bytes 1474560 | tf_op jit(solution)/shard_map/reduce_scatter | solution.py:136
  356.6 68.5 %all-gather.16.cloned.1.call-start = ((), (), s32[]{:S(2)}) async-start(), calls=%async_computation.15 | async-start | bytes 1474560 | tf_op jit(solution)/shard_map/all_gather | solution.py:141
  407.6 92.5 %reduce-scatter.22.cloned.1.call-start = ((), (), s32[]{:S(2)}) async-start(), calls=%async_computation.18 | async-start | bytes 2985984 | tf_op jit(solution)/shard_map/reduce_scatter | solution.py:353
  412.6 161.8 %reduce-scatter.24.cloned.1.call-start = ((), (), s32[]{:S(2)}) async-start(), calls=%async_computation.19 | async-start | bytes 2985984 | tf_op jit(solution)/shard_map/reduce_scatter | solution.py:356
  418.1 221.5 %reduce-scatter.20.cloned.1.call-start = ((), (), s32[]{:S(2)}) async-start(), calls=%async_computation.17 | async-start | bytes 995328 | tf_op jit(solution)/shard_map/reduce_scatter | solution.py:350
  438.9 227.5 %reduce-scatter.18.cloned.1.call-start = ((), (), s32[]{:S(2)}) async-start(), calls=%async_computation.16 | async-start | bytes 1474560 | tf_op jit(solution)/shard_map/reduce_scatter | solution.py:144
  443.4 5.1 copy-start.15
  452.3 328.0 %reduce-scatter.26.cloned.1.call-start = ((), (), s32[]{:S(2)}) async-start(), calls=%async_computation.22 | async-start | bytes 2322432
  466.7 7.5 copy-start.48
  466.7 7.6 copy-start.45
  474.4 196.0 %copy-start.17 = (bf16[128,1152]{1,0:T(8,128)(2,1)S(1)}, bf16[128,1152]{1,0:T(8,128)(2,1)}, u32[]{:S(2)}) copy-start(bf16[128,1152]{1,0:T(8,128)(2,1)} %reduce-scatter.12.cloned.1.call-done) | copy-start | bytes 884740
  474.4 197.7 %copy-start.10 = (bf16[128,1152]{1,0:T(8,128)(2,1)S(1)}, bf16[128,1152]{1,0:T(8,128)(2,1)}, u32[]{:S(2)}) copy-start(bf16[128,1152]{1,0:T(8,128)(2,1)} %reduce-scatter.16.cloned.1.call-done) | copy-start | bytes 884740
  474.6 166.5 %copy-start.33 = (f32[1,2,1152]{2,1,0:T(2,128)}, f32[1,2,1152]{2,1,0:T(2,128)S(1)}, u32[]{:S(2)}) copy-start(f32[1,2,1152]{2,1,0:T(2,128)S(1)} %dynamic_update_slice.8) | copy-start | bytes 27652
  501.9 173.4 %copy-start.18 = (bf16[128,1152]{1,0:T(8,128)(2,1)S(1)}, bf16[128,1152]{1,0:T(8,128)(2,1)}, u32[]{:S(2)}) copy-start(bf16[128,1152]{1,0:T(8,128)(2,1)} %reduce-scatter.14.cloned.1.call-done) | copy-start | bytes 884740
  666.4 12.2 %copy-start.6 = (bf16[128,1152]{1,0:T(8,128)(2,1)S(1)}, bf16[128,1152]{1,0:T(8,128)(2,1)}, u32[]{:S(2)}) copy-start(bf16[128,1152]{1,0:T(8,128)(2,1)} %reduce-scatter.18.cloned.1.call-done) | copy-start | bytes 884740
  676.5 46.1 %copy-start.16 = (bf16[1,144,1728]{2,1,0:T(8,128)(2,1)S(1)}, bf16[1,144,1728]{2,1,0:T(8,128)(2,1)}, u32[]{:S(2)}) copy-start(bf16[1,144,1728]{2,1,0:T(8,128)(2,1)} %param.21) | copy-start | bytes 1492996
  678.6 55.4 %copy-start.32 = (f32[1,4608]{1,0:T(1,128)S(1)}, f32[1,4608]{1,0:T(1,128)}, u32[]{:S(2)}) copy-start(f32[1,4608]{1,0:T(1,128)} %copy-done.31) | copy-start | bytes 55300
  678.6 55.4 %copy-start.34 = (f32[1,2,1152]{2,1,0:T(2,128)S(1)}, f32[1,2,1152]{2,1,0:T(2,128)}, u32[]{:S(2)}) copy-start(f32[1,2,1152]{2,1,0:T(2,128)} %copy-done.33) | copy-start | bytes 27652
  678.6 97.2 %copy-start.28 = (f32[16,128]{1,0:T(8,128)S(1)}, f32[16,128]{1,0:T(8,128)}, u32[]{:S(2)}) copy-start(f32[16,128]{1,0:T(8,128)} %copy-done.27) | copy-start | bytes 24580
  678.7 97.1 %copy-start.30 = (f32[16,128]{1,0:T(8,128)S(1)}, f32[16,128]{1,0:T(8,128)}, u32[]{:S(2)}) copy-start(f32[16,128]{1,0:T(8,128)} %copy-done.29) | copy-start | bytes 24580
  678.7 98.2 %copy-start.49 = (s32[16]{0:T(128)S(1)}, s32[16]{0:T(128)}, u32[]{:S(2)}) copy-start(s32[16]{0:T(128)} %param.18) | copy-start | bytes 196
  680.4 97.7 %copy-start.39 = (f32[128]{0:T(128)S(1)}, f32[128]{0:T(128)}, u32[]{:S(2)}) copy-start(f32[128]{0:T(128)} %copy-done.38) | copy-start | bytes 1540
  680.4 97.7 %copy-start.43 = (f32[128]{0:T(128)S(1)}, f32[128]{0:T(128)}, u32[]{:S(2)}) copy-start(f32[128]{0:T(128)} %copy-done.42) | copy-start | bytes 1540
  778.1 5.4 copy-start.1
  (21 other events, 61.7 us)
Sparse Core Ops, SparseCore 0:
  12.7 72.4 all-reduce.3
  115.8 16.3 all-gather.9
  134.5 55.3 all-gather.17
  204.7 24.1 reduce-scatter.11
  230.9 71.9 all-gather.19
  304.9 16.2 all-gather.11
  323.3 17.4 all-gather.13
  351.0 25.5 reduce-scatter.15
  379.2 25.6 reduce-scatter.13
  407.7 17.4 all-gather.15
  428.8 71.2 reduce-scatter.21
  503.6 70.7 reduce-scatter.23
  578.4 61.1 reduce-scatter.19
  642.0 24.3 reduce-scatter.17
  669.8 68.2 reduce-scatter.25
